TPU v7x, 32 devices: a whole 2x2x4 slice. The times are simulated.
32 devices in a mesh: dp: 8 (over z, y), tensor: 4 (over x, core).
Axes of the slice: x: 2, y: 2, z: 4, core: 2. Of those that a mesh axis runs over, the one named last changes fastest.
Arguments:
- query: bfloat16 [64, 64, 128], P('dp', 'tensor'), may hold values from -8 to 8
- kv_pages: bfloat16 [560, 8, 2, 128, 128], P('dp', 'tensor'), may hold values from -8 to 8
- move_plan: int32 [8, 3, 12], P('dp'), may hold values from 0 to 69, as said below
- move_count: int32 [8], P('dp'), may hold values from 9 to 12
- block_table: int32 [64, 8], P('dp'), may hold values from 0 to 69, as said below
- seq_lens: int32 [64], P('dp'), may hold values from 1 to 1024
- out_weight: bfloat16 [8192, 8192], P('tensor', 'dp'), may hold values from -0.0625 to 0.0625
Outputs:
- new_pages: bfloat16 [560, 8, 2, 128, 128], P('dp', 'tensor')
- projected: bfloat16 [64, 8192], P(None, 'dp')
Inputs may be any that keep to these rules, and one draw needn't show every extreme that they name: `move_plan`: row 0 holds the device's own source slots, distinct within a device; row 1 target devices; row 2 target slots. Entries at or past the device's move_count are padding to be ignored. At most 2 valid moves go from one device to one device, and some pair has exactly 2. The (target device, target slot) pairs of all valid moves are distinct. `block_table`: all entries of the sequences of one device are distinct slots of that device; sequence s belongs to device s // 8.
All inputs are finite; a program needn't handle non-finite values.
Results may differ from a plain program's by a relative error of at most 0.0055.
Values may be sent and summed in bfloat16 or wider, within the bound.
No kernel may reach another device: no remote copies, remote signals or barrier semaphores. Data moves between devices by JAX's collectives and lax.ppermute only.
A program may use at most 128 MiB of HBM per device.

v0:
```python
import math
import jax
import jax.numpy as jnp
from jax import lax
from jax.sharding import PartitionSpec as P

HD = 128
BLOCK = 128
BLOCKS = 8
CAP = 2


def body(query, kv_pages, move_plan, move_count, block_table, seq_lens, out_weight):
    slots_here = kv_pages.shape[0]
    move_total = move_plan.shape[2]
    devices = lax.axis_size("dp")
    capacity = CAP
    holding_rows = devices * capacity
    move_list = move_plan[0]
    move_index = jnp.arange(move_total, dtype=jnp.int32)
    is_valid = move_index < move_count[0]
    target_dev = move_list[1]
    earlier = (
        (target_dev[:, None] == target_dev[None, :])
        & is_valid[None, :]
        & (move_index[None, :] < move_index[:, None])
    )
    dest_rank = jnp.sum(earlier.astype(jnp.int32), axis=1)
    send_row = jnp.where(is_valid, target_dev * capacity + dest_rank, -1)
    flat_pages = kv_pages.reshape(slots_here, -1)
    picked = flat_pages[move_list[0]]
    select = jnp.arange(holding_rows, dtype=jnp.int32)[:, None] == send_row[None, :]
    outgoing = jnp.dot(
        select.astype(jnp.bfloat16), picked, preferred_element_type=jnp.float32
    ).astype(jnp.bfloat16)
    outgoing = outgoing.reshape((holding_rows,) + kv_pages.shape[1:])
    out_slots = jnp.sum(select.astype(jnp.int32) * (move_list[2][None, :] + 1), axis=1) - 1
    slot_tags = out_slots.astype(jnp.float32).astype(jnp.bfloat16)
    arrived, arrived_tags = (
        lax.all_to_all(outgoing, "dp", split_axis=0, concat_axis=0, tiled=True),
        lax.all_to_all(slot_tags, "dp", split_axis=0, concat_axis=0, tiled=True),
    )
    incoming = arrived_tags.astype(jnp.float32).astype(jnp.int32)
    hit_table = jnp.arange(slots_here, dtype=jnp.int32)[:, None] == incoming[None, :]
    placed = jnp.dot(
        hit_table.astype(jnp.bfloat16),
        arrived.reshape(holding_rows, -1),
        preferred_element_type=jnp.float32,
    ).astype(jnp.bfloat16)
    written = jnp.any(hit_table, axis=1)
    new_pages = jnp.where(written[:, None], placed, flat_pages).reshape(kv_pages.shape)
    seq_here = query.shape[0]
    local_heads = new_pages.shape[1]
    head_dim = query.shape[2]
    group_size = query.shape[1] // local_heads
    context = BLOCKS * BLOCK
    gathered = new_pages[block_table]
    key_rows = jnp.transpose(gathered[:, :, :, 0], (0, 2, 1, 3, 4)).reshape(
        seq_here, local_heads, context, head_dim
    )
    value_rows = jnp.transpose(gathered[:, :, :, 1], (0, 2, 1, 3, 4)).reshape(
        seq_here, local_heads, context, head_dim
    )
    grouped = query.reshape(seq_here, local_heads, group_size, head_dim)
    score_scale = 1.0 / math.sqrt(HD)
    scores = (
        jnp.einsum("skgd,sktd->skgt", grouped, key_rows, preferred_element_type=jnp.float32)
        * score_scale
    )
    position = jnp.arange(context, dtype=jnp.int32)
    scores = jnp.where(position[None, None, None, :] < seq_lens[:, None, None, None], scores, -1e30)
    largest = jnp.max(scores, axis=-1, keepdims=True)
    expo = jnp.exp(scores - largest)
    weights = (expo / jnp.sum(expo, axis=-1, keepdims=True)).astype(jnp.bfloat16)
    mixed_heads = jnp.einsum(
        "skgt,sktd->skgd", weights, value_rows, preferred_element_type=jnp.float32
    )
    attention = mixed_heads.reshape(seq_here, local_heads * group_size * head_dim).astype(
        jnp.bfloat16
    )
    partial_sums = jnp.dot(
        lax.all_gather(attention, "dp", axis=0, tiled=True),
        out_weight,
        preferred_element_type=jnp.float32,
    )
    summed = lax.psum(partial_sums, "tensor")
    return (new_pages, summed.astype(jnp.bfloat16))


def solution(mesh):
    placed = (
        P("dp", "tensor", None),
        P("dp", "tensor", None, None, None),
        P("dp", None, None),
        P("dp"),
        P("dp", None),
        P("dp"),
        P("tensor", "dp"),
    )
    return jax.shard_map(
        body,
        mesh=mesh,
        in_specs=placed,
        out_specs=(P("dp", "tensor", None, None, None), P(None, "dp")),
        check_vma=False,
    )
```

profile of v0, /device:TPU:1, one launch (start us, length us, event | category | flops | bytes accessed | tf_op | source)
XLA Modules:
  0.0 194.9 jit_solution(8297206147046076033)
XLA Ops:
  0.6 0.7 slice_bitcast_fusion
  2.2 0.7 add_select_fusion
  3.0 0.7 convert_element_type.79
  3.7 6.4 %all-to-all-start = ((bf16[8,2,1]{1,2,0:T(2,128)(2,1)}), bf16[8,2,1]{1,2,0:T(2,128)(2,1)S(1)}, u32[]{:S(2)}, u32[]{:S(2)}) async-start(bf16[8,2,1]{1,2,0:T(2,128)(2,1)} %convert_element_type.79), calls=%async_computation | async-start | bytes 8192 | tf_op jit(solution)/shard_map/all_to_all | solution.py:41
  10.0 0.7 fusion.16
  10.7 8.8 %pad.2 = bf16[72,512,128]{2,1,0:T(8,128)(2,1)} pad(bf16[70,512,128]{2,1,0:T(8,128)(2,1)} %bitcast.69, bf16[]{:T(256)} %constant.38), padding=0_2x0_0x0_0 | pad | bytes 18612226
  19.5 13.8 %copy.21 = bf16[9,8,512,128]{3,1,2,0:T(8,128)(2,1)} copy(bf16[9,8,512,128]{3,2,1,0:T(8,128)(2,1)} %bitcast.62) | data formatting | bytes 18874368
  33.3 7.8 %gather_fusion = bf16[12,65536]{1,0:T(8,128)(2,1)S(1)} fusion(bf16[70,65536]{1,0:T(8,128)(2,1)} %bitcast.59, s32[1024]{0:T(1024)S(1)} %pad_clamp_fusion.1), kind=kCustom, calls=%fused_computation | custom fusion | bytes 3145776 | tf_op jit(solution)/shard_map/gather | solution.py:31
  41.1 0.7 fusion.4
  41.8 1.9 copy.22
  43.7 5.4 %all-to-all-start.1 = ((bf16[16,2,2,128,128]{4,3,2,1,0:T(8,128)(2,1)}), bf16[16,2,2,128,128]{4,3,2,1,0:T(8,128)(2,1)S(1)}, u32[]{:S(2)}, u32[]{:S(2)}) async-start(bf16[16,2,2,128,128]{4,3,2,1,0:T(8,128)(2,1)} %bitcast.24), calls=%async_computation.1 | async-start | bytes 4194304 | tf_op jit(solution)/shard_map/all_to_all | solution.py:40
  49.5 46.5 %all-to-all-done.1 = bf16[16,2,2,128,128]{4,3,2,1,0:T(8,128)(2,1)S(1)} async-done(((bf16[16,2,2,128,128]{4,3,2,1,0:T(8,128)(2,1)}), bf16[16,2,2,128,128]{4,3,2,1,0:T(8,128)(2,1)S(1)}, u32[]{:S(2)}, u32[]{:S(2)}) %all-to-all-start.1) | async-done | bytes 2097184 | tf_op jit(solution)/shard_map/all_to_all | solution.py:40
  96.0 10.8 %fusion.1 = bf16[70,65536]{1,0:T(8,128)(2,1)} fusion(bf16[70,65536]{1,0:T(8,128)(2,1)} %bitcast.60, pred[70]{0:T(512)(128)(4,1)S(1)} %fusion.12, bf16[2,8,512,128]{3,2,1,0:T(8,128)(2,1)S(1)} %bitcast.70, s32[16]{0:T(128)S(1)} %convert_element_type.72), kind=kOutput, calls=%fused_computation.4 | convolution fusion | flops 155976800 | bytes 20447366 | tf_op jit(solution)/shard_map/dot_general | solution.py:45
  106.8 9.9 %copy.24 = bf16[9,8,512,128]{3,2,1,0:T(8,128)(2,1)} copy(bf16[9,8,512,128]{3,1,2,0:T(8,128)(2,1)} %bitcast.61) | data formatting | bytes 18874368
  116.7 8.4 %slice.29 = bf16[70,512,128]{2,1,0:T(8,128)(2,1)} slice(bf16[72,512,128]{2,1,0:T(8,128)(2,1)} %bitcast.63), slice={[0:70], [0:512], [0:128]} | slice | bytes 18350080
  125.1 9.1 %gather_fusion.1 = bf16[64,2,2,128,128]{4,3,2,1,0:T(8,128)(2,1)} fusion(bf16[70,2,2,128,128]{4,3,2,1,0:T(8,128)(2,1)} %bitcast.64, s32[1024]{0:T(1024)S(1)} %pad_clamp_fusion), kind=kCustom, calls=%fused_computation.1 | custom fusion | bytes 16777472 | tf_op jit(solution)/shard_map/gather | solution.py:57
  134.2 3.8 %fusion.17 = (bf16[8,8,2,1,128,128]{5,4,3,2,1,0:T(8,128)(2,1)S(1)}, bf16[8,8,2,1,128,128]{5,4,3,2,1,0:T(8,128)(2,1)S(1)}) fusion(bf16[8,8,2,2,128,128]{5,4,3,2,1,0:T(8,128)(2,1)} %bitcast.66), kind=kLoop, calls=%fused_computation.41 | loop fusion | bytes 16777216 | tf_op jit(solution)/shard_map/slice | solution.py:58
  138.1 0.6 copy.19
  138.7 1.2 fusion.8
  140.1 2.2 %copy.20 = bf16[8,8,2,1,128,128]{5,4,1,2,0,3:T(8,128)(2,1)} copy(bf16[8,8,2,1,128,128]{5,4,3,2,1,0:T(8,128)(2,1)S(1)} %get-tuple-element.3) | data formatting | bytes 8388608
  142.3 2.9 %fusion.9 = bf16[1,8,16,128]{3,2,1,0:T(8,128)(2,1)S(1)} fusion(bf16[8,2,1024,128]{3,2,1,0:T(8,128)(2,1)} %bitcast.67, f32[8,2,8]{2,1,0:T(2,128)S(1)} %fusion.18, f32[8,2,8,1024]{3,2,1,0:T(8,128)S(1)} %fusion.8), kind=kOutput, calls=%fused_computation.15 | convolution fusion | flops 33965184 | bytes 4751872 | tf_op jit(solution)/shard_map/skgt,sktd->skgd/dot_general | solution.py:75
  145.3 25.4 %all_gather.3 = bf16[64,2048]{1,0:T(8,128)(2,1)S(1)} all-gather(bf16[8,2048]{1,0:T(8,128)(2,1)S(1)} %bitcast.71), channel_id=1, replica_groups=mesh['dp'=8,'tensor'=4] {'dp'}, dimensions={0}, use_global_device_ids=true | all-gather | bytes 294912 | tf_op jit(solution)/shard_map/all_gather | solution.py:82
  170.7 3.0 %fusion.19 = f32[64,1024]{1,0:T(8,128)S(1)} fusion(bf16[64,2048]{1,0:T(8,128)(2,1)S(1)} %all_gather.3, bf16[2048,1024]{1,0:T(8,128)(2,1)} %param.13), kind=kOutput, calls=%fused_computation.43 | convolution fusion | flops 268435456 | bytes 4718592 | tf_op jit(solution)/shard_map/dot_general | solution.py:81
  173.7 21.2 %all-reduce.1 = bf16[64,1024]{1,0:T(8,128)(2,1)} all-reduce(f32[64,1024]{1,0:T(8,128)S(1)} %fusion.19), channel_id=1, replica_groups=mesh['dp'=8,'tensor'=4] {'tensor'}, use_global_device_ids=true, to_apply=%region_5.6 | all-reduce | flops 65536 | bytes 393216 | tf_op jit(solution)/shard_map/psum | solution.py:86
  (21 shorter events, 1.0 us)
Async XLA Ops:
  0.6 138.0 %copy-start = (bf16[8,16,128]{2,1,0:T(8,128)(2,1)S(1)}, bf16[8,16,128]{2,1,0:T(8,128)(2,1)}, u32[]{:S(2)}) copy-start(bf16[8,16,128]{2,1,0:T(8,128)(2,1)} %param.7) | copy-start | bytes 98308
  3.7 40.1 %all-to-all-start = ((bf16[8,2,1]{1,2,0:T(2,128)(2,1)}), bf16[8,2,1]{1,2,0:T(2,128)(2,1)S(1)}, u32[]{:S(2)}, u32[]{:S(2)}) async-start(bf16[8,2,1]{1,2,0:T(2,128)(2,1)} %convert_element_type.79), calls=%async_computation | async-start | bytes 8192 | tf_op jit(solution)/shard_map/all_to_all | solution.py:41
  41.8 7.3 %copy-start.1 = (s32[8,8]{1,0:T(8,128)S(1)}, s32[8,8]{1,0:T(8,128)}, u32[]{:S(2)}) copy-start(s32[8,8]{1,0:T(8,128)} %param.11) | copy-start | bytes 772
  41.8 7.4 %copy-start.2 = (s32[8]{0:T(128)S(1)}, s32[8]{0:T(128)}, u32[]{:S(2)}) copy-start(s32[8]{0:T(128)} %param.12) | copy-start | bytes 100
  43.7 52.3 %all-to-all-start.1 = ((bf16[16,2,2,128,128]{4,3,2,1,0:T(8,128)(2,1)}), bf16[16,2,2,128,128]{4,3,2,1,0:T(8,128)(2,1)S(1)}, u32[]{:S(2)}, u32[]{:S(2)}) async-start(bf16[16,2,2,128,128]{4,3,2,1,0:T(8,128)(2,1)} %bitcast.24), calls=%async_computation.1 | async-start | bytes 4194304 | tf_op jit(solution)/shard_map/all_to_all | solution.py:40
where the time goes:
time: 196 us; the launch traced here: 195 us
  local copies, waits for them, and re-layouts  67.2 us (34%)
  blocking collectives  46.6 us (24%)
  waiting for transfers between devices  46.5 us (24%)
  matrix products  18.6 us (9%)
  starting transfers between devices  11.8 us (6%)
  other arithmetic  2.78 us (1%)
    all_to_all x1, waiting for transfers between devices, body(): lax.all_to_all(outgoing, 'dp', split_axis=0, concat_axis=0, tiled=True)  46.5 us
    unnamed x14, local copies, waits for them, and re-layouts  45.6 us
    all_gather x1, blocking collectives, body(): lax.all_gather(attention, 'dp', axis=0, tiled=True)  25.4 us
    psum x1, blocking collectives, body(): summed = lax.psum(partial_sums, 'tensor')  21.2 us
    dot_general x1, matrix products, body(): jnp.dot(hit_table.astype(jnp.bfloat16), arrived.reshape(holding_rows, -1)...  10.8 us
    gather x1, local copies, waits for them, and re-layouts, body(): gathered = new_pages[block_table]  9.14 us
    gather x1, local copies, waits for them, and re-layouts, body(): picked = flat_pages[move_list[0]]  7.81 us
    all_to_all x1, starting transfers between devices, body(): lax.all_to_all(slot_tags, 'dp', split_axis=0, concat_axis=0, tiled=True)  6.37 us
  transfers between devices with their start and end apart: 2, of which 1 were waited for; matrix products, arithmetic and copies ran while one was open for 17% of the time, Pallas kernels for 0%

commit v1 on v0

--- a/solution.py
+++ b/solution.py
@@ -83,7 +83,7 @@
         out_weight,
         preferred_element_type=jnp.float32,
     )
-    summed = lax.psum(partial_sums, "tensor")
+    summed = jnp.sum(lax.all_gather(partial_sums, "tensor"), axis=0)
     return (new_pages, summed.astype(jnp.bfloat16))
 
 

time: 196 us -> 214 us (1.092)
  waiting for transfers between devices: 46.5 us -> 69.8 us
  blocking collectives: 46.6 us -> 25.4 us
  between operations: 1.4 us -> 14.8 us
    all_gather x0 -> x1, waiting for transfers between devices: none -> 23.4 us  [body(): summed = jnp.sum(lax.all_gather(partial_sums, 'tensor'), axis=0)]
    psum x1 -> x0, blocking collectives: 21.2 us -> none  [body(): summed = lax.psum(partial_sums, 'tensor')]
  transfers between devices with their start and end apart: 2 -> 3, of which waited for: 1 -> 2; matrix products, arithmetic and copies ran while one was open for 17% -> 16% of each run, Pallas kernels for 0% -> 0%
where the time goes in v1:
time: 214 us; the launch traced here: 213 us
  waiting for transfers between devices  69.8 us (33%)
  local copies, waits for them, and re-layouts  67.2 us (31%)
  blocking collectives  25.4 us (12%)
  matrix products  19.3 us (9%)
  between operations  14.8 us (7%)
  starting transfers between devices  11.8 us (6%)
  other arithmetic  4.76 us (2%)
    all_to_all x1, waiting for transfers between devices, body(): lax.all_to_all(outgoing, 'dp', split_axis=0, concat_axis=0, tiled=True)  46.4 us
    unnamed x14, local copies, waits for them, and re-layouts  45.6 us
    all_gather x1, blocking collectives, body(): lax.all_gather(attention, 'dp', axis=0, tiled=True)  25.4 us
    all_gather x1, waiting for transfers between devices, body(): summed = jnp.sum(lax.all_gather(partial_sums, 'tensor'), axis=0)  23.4 us
    dot_general x1, matrix products, body(): jnp.dot(hit_table.astype(jnp.bfloat16), arrived.reshape(holding_rows, -1)...  10.8 us
    gather x1, local copies, waits for them, and re-layouts, body(): gathered = new_pages[block_table]  9.14 us
    gather x1, local copies, waits for them, and re-layouts, body(): picked = flat_pages[move_list[0]]  7.81 us
    all_to_all x1, starting transfers between devices, body(): lax.all_to_all(slot_tags, 'dp', split_axis=0, concat_axis=0, tiled=True)  6.37 us
  transfers between devices with their start and end apart: 3, of which 2 were waited for; matrix products, arithmetic and copies ran while one was open for 16% of the time, Pallas kernels for 0%

profile of v1, /device:TPU:1, one launch (start us, length us, event | category | flops | bytes accessed | tf_op | source)
XLA Modules:
  0.0 213.2 jit_solution(12264082250084426535)
XLA Ops:
  7.2 0.7 slice_bitcast_fusion
  8.7 0.7 add_select_fusion
  9.5 0.7 convert_element_type.79
  10.2 6.4 %all-to-all-start = ((bf16[8,2,1]{1,2,0:T(2,128)(2,1)}), bf16[8,2,1]{1,2,0:T(2,128)(2,1)S(1)}, u32[]{:S(2)}, u32[]{:S(2)}) async-start(bf16[8,2,1]{1,2,0:T(2,128)(2,1)} %convert_element_type.79), calls=%async_computation | async-start | bytes 8192 | tf_op jit(solution)/shard_map/all_to_all | solution.py:41
  16.6 0.7 fusion.16
  17.2 8.8 %pad.2 = bf16[72,512,128]{2,1,0:T(8,128)(2,1)} pad(bf16[70,512,128]{2,1,0:T(8,128)(2,1)} %bitcast.70, bf16[]{:T(256)} %constant.38), padding=0_2x0_0x0_0 | pad | bytes 18612226
  26.0 13.8 %copy.21 = bf16[9,8,512,128]{3,1,2,0:T(8,128)(2,1)} copy(bf16[9,8,512,128]{3,2,1,0:T(8,128)(2,1)} %bitcast.63) | data formatting | bytes 18874368
  39.8 7.8 %gather_fusion = bf16[12,65536]{1,0:T(8,128)(2,1)S(1)} fusion(bf16[70,65536]{1,0:T(8,128)(2,1)} %bitcast.60, s32[1024]{0:T(1024)S(1)} %pad_clamp_fusion.1), kind=kCustom, calls=%fused_computation | custom fusion | bytes 3145776 | tf_op jit(solution)/shard_map/gather | solution.py:31
  47.7 0.7 fusion.4
  48.4 1.9 copy.22
  50.2 5.4 %all-to-all-start.1 = ((bf16[16,2,2,128,128]{4,3,2,1,0:T(8,128)(2,1)}), bf16[16,2,2,128,128]{4,3,2,1,0:T(8,128)(2,1)S(1)}, u32[]{:S(2)}, u32[]{:S(2)}) async-start(bf16[16,2,2,128,128]{4,3,2,1,0:T(8,128)(2,1)} %bitcast.25), calls=%async_computation.1 | async-start | bytes 4194304 | tf_op jit(solution)/shard_map/all_to_all | solution.py:40
  56.1 46.4 %all-to-all-done.1 = bf16[16,2,2,128,128]{4,3,2,1,0:T(8,128)(2,1)S(1)} async-done(((bf16[16,2,2,128,128]{4,3,2,1,0:T(8,128)(2,1)}), bf16[16,2,2,128,128]{4,3,2,1,0:T(8,128)(2,1)S(1)}, u32[]{:S(2)}, u32[]{:S(2)}) %all-to-all-start.1) | async-done | bytes 2097184 | tf_op jit(solution)/shard_map/all_to_all | solution.py:40
  102.6 10.8 %fusion.1 = bf16[70,65536]{1,0:T(8,128)(2,1)} fusion(bf16[70,65536]{1,0:T(8,128)(2,1)} %bitcast.61, pred[70]{0:T(512)(128)(4,1)S(1)} %fusion.12, bf16[2,8,512,128]{3,2,1,0:T(8,128)(2,1)S(1)} %bitcast.71, s32[16]{0:T(128)S(1)} %convert_element_type.72), kind=kOutput, calls=%fused_computation.4 | convolution fusion | flops 155976800 | bytes 20447366 | tf_op jit(solution)/shard_map/dot_general | solution.py:45
  113.3 9.9 %copy.24 = bf16[9,8,512,128]{3,2,1,0:T(8,128)(2,1)} copy(bf16[9,8,512,128]{3,1,2,0:T(8,128)(2,1)} %bitcast.62) | data formatting | bytes 18874368
  123.3 8.4 %slice.29 = bf16[70,512,128]{2,1,0:T(8,128)(2,1)} slice(bf16[72,512,128]{2,1,0:T(8,128)(2,1)} %bitcast.64), slice={[0:70], [0:512], [0:128]} | slice | bytes 18350080
  131.6 9.1 %gather_fusion.1 = bf16[64,2,2,128,128]{4,3,2,1,0:T(8,128)(2,1)} fusion(bf16[70,2,2,128,128]{4,3,2,1,0:T(8,128)(2,1)} %bitcast.65, s32[1024]{0:T(1024)S(1)} %pad_clamp_fusion), kind=kCustom, calls=%fused_computation.1 | custom fusion | bytes 16777472 | tf_op jit(solution)/shard_map/gather | solution.py:57
  140.8 3.8 %fusion.17 = (bf16[8,8,2,1,128,128]{5,4,3,2,1,0:T(8,128)(2,1)S(1)}, bf16[8,8,2,1,128,128]{5,4,3,2,1,0:T(8,128)(2,1)S(1)}) fusion(bf16[8,8,2,2,128,128]{5,4,3,2,1,0:T(8,128)(2,1)} %bitcast.67), kind=kLoop, calls=%fused_computation.41 | loop fusion | bytes 16777216 | tf_op jit(solution)/shard_map/slice | solution.py:58
  145.2 1.2 fusion.8
  146.6 2.2 %copy.20 = bf16[8,8,2,1,128,128]{5,4,1,2,0,3:T(8,128)(2,1)} copy(bf16[8,8,2,1,128,128]{5,4,3,2,1,0:T(8,128)(2,1)S(1)} %get-tuple-element.3) | data formatting | bytes 8388608
  148.9 2.9 %fusion.9 = bf16[1,8,16,128]{3,2,1,0:T(8,128)(2,1)S(1)} fusion(bf16[8,2,1024,128]{3,2,1,0:T(8,128)(2,1)} %bitcast.68, f32[8,2,8]{2,1,0:T(2,128)S(1)} %fusion.18, f32[8,2,8,1024]{3,2,1,0:T(8,128)S(1)} %fusion.8), kind=kOutput, calls=%fused_computation.15 | convolution fusion | flops 33965184 | bytes 4751872 | tf_op jit(solution)/shard_map/skgt,sktd->skgd/dot_general | solution.py:75
  151.8 25.4 %all_gather.9 = bf16[64,2048]{1,0:T(8,128)(2,1)S(1)} all-gather(bf16[8,2048]{1,0:T(8,128)(2,1)S(1)} %bitcast.73), channel_id=1, replica_groups=mesh['dp'=8,'tensor'=4] {'dp'}, dimensions={0}, use_global_device_ids=true | all-gather | bytes 294912 | tf_op jit(solution)/shard_map/all_gather | solution.py:82
  177.2 3.8 %fusion.19 = f32[64,1024]{1,0:T(8,128)} fusion(bf16[64,2048]{1,0:T(8,128)(2,1)S(1)} %all_gather.9, bf16[2048,1024]{1,0:T(8,128)(2,1)} %param.13), kind=kOutput, calls=%fused_computation.43 | convolution fusion | flops 268435456 | bytes 4718592 | tf_op jit(solution)/shard_map/dot_general | solution.py:81
  181.0 23.4 %all-gather.3.cloned.1.call-done = f32[256,1024]{1,0:T(8,128)} async-done(((f32[64,1024]{1,0:T(8,128)}), f32[256,1024]{1,0:T(8,128)}) %all-gather.3.cloned.1.call-update) | async-done | bytes 1048592 | tf_op jit(solution)/shard_map/all_gather | solution.py:86
  204.4 2.0 reduce_sum.39
  (24 shorter events, 1.6 us)
Async XLA Ops:
  7.2 138.0 %copy-start = (bf16[8,16,128]{2,1,0:T(8,128)(2,1)S(1)}, bf16[8,16,128]{2,1,0:T(8,128)(2,1)}, u32[]{:S(2)}) copy-start(bf16[8,16,128]{2,1,0:T(8,128)(2,1)} %param.7) | copy-start | bytes 98308
  10.2 40.1 %all-to-all-start = ((bf16[8,2,1]{1,2,0:T(2,128)(2,1)}), bf16[8,2,1]{1,2,0:T(2,128)(2,1)S(1)}, u32[]{:S(2)}, u32[]{:S(2)}) async-start(bf16[8,2,1]{1,2,0:T(2,128)(2,1)} %convert_element_type.79), calls=%async_computation | async-start | bytes 8192 | tf_op jit(solution)/shard_map/all_to_all | solution.py:41
  48.3 7.4 %copy-start.1 = (s32[8,8]{1,0:T(8,128)S(1)}, s32[8,8]{1,0:T(8,128)}, u32[]{:S(2)}) copy-start(s32[8,8]{1,0:T(8,128)} %param.11) | copy-start | bytes 772
  48.4 7.5 %copy-start.2 = (s32[8]{0:T(128)S(1)}, s32[8]{0:T(128)}, u32[]{:S(2)}) copy-start(s32[8]{0:T(128)} %param.12) | copy-start | bytes 100
  50.2 52.3 %all-to-all-start.1 = ((bf16[16,2,2,128,128]{4,3,2,1,0:T(8,128)(2,1)}), bf16[16,2,2,128,128]{4,3,2,1,0:T(8,128)(2,1)S(1)}, u32[]{:S(2)}, u32[]{:S(2)}) async-start(bf16[16,2,2,128,128]{4,3,2,1,0:T(8,128)(2,1)} %bitcast.25), calls=%async_computation.1 | async-start | bytes 4194304 | tf_op jit(solution)/shard_map/all_to_all | solution.py:40
  55.7 148.7 %all-gather.3.cloned.1.call-start = ((), (), s32[]{:S(2)}) async-start(), calls=%async_computation.2 | async-start | bytes 1310720 | tf_op jit(solution)/shard_map/all_gather | solution.py:86
Sparse Core Ops, SparseCore 0:
  181.1 23.2 all-gather.2
